TPU v7x, 32 devices: a whole 2x2x4 slice. The times are simulated.
32 devices in a mesh: groups: 2 (over x), queue: 16 (over z, y, core).
Axes of the slice: x: 2, y: 2, z: 4, core: 2. Of those that a mesh axis runs over, the one named last changes fastest.
Arguments:
- hidden: bfloat16 [256, 5120], P(('groups', 'queue')), parts along dimension 0, may hold values from -6 to 6
- incoming: bfloat16 [2, 16, 5120], P(None, 'groups'), parts along dimension 1, may hold values from -6 to 6
- levels: int32 [16], replicated, may hold values from 0 to 95, as said below
- mod_table: bfloat16 [96, 3, 5120], replicated, may hold values from -3 to 3
- query_weight: bfloat16 [5120, 5120], P(None, 'queue'), may hold values from -0.078125 to 0.078125
- key_weight: bfloat16 [5120, 5120], P(None, 'queue'), may hold values from -0.078125 to 0.078125
- value_weight: bfloat16 [5120, 5120], P(None, 'queue'), may hold values from -0.078125 to 0.078125
- output_weight: bfloat16 [5120, 5120], P(None, 'queue'), may hold values from -0.078125 to 0.078125
- query_gain: float32 [5120], replicated, may hold values from 0.5 to 1.5
- key_gain: float32 [5120], replicated, may hold values from 0.5 to 1.5
- text_keys: bfloat16 [1024, 5120], P(('groups', 'queue')), parts along dimension 0, may hold values from -6 to 6
- text_values: bfloat16 [1024, 5120], P(('groups', 'queue')), parts along dimension 0, may hold values from -6 to 6
Outputs:
- updated: bfloat16 [256, 5120], P(('groups', 'queue')), parts along dimension 0
There are 2 independent parts, one for each index of `groups`. A program takes and returns all parts, laid end to end along the dimension named above; an argument that names none is the same for every part. Nothing has to cross between parts.
Inputs may be any that keep to these rules, and one draw needn't show every extreme that they name: `levels`: strictly rising along the queue positions; the last position always has level 95.
All inputs are finite; a program needn't handle non-finite values.
Results may differ from a plain program's by a relative error of at most 0.0085.
Values may be sent and summed in bfloat16 or wider, within the bound.
A program may use at most 128 MiB of HBM per device.

v0:
```python
import math

import jax
import jax.numpy as jnp
from jax import lax
from jax.sharding import PartitionSpec as P

HEADS = 40
STEPS = 2


def passed_along(value, axis, steps):
    count = lax.axis_size(axis)
    initial, last = (max(0, -steps), min(count, count - steps))
    return lax.ppermute(value, axis, [(source, source + steps) for source in range(initial, last)])


def normalize(values):
    return values * lax.rsqrt(jnp.mean(values * values, axis=-1, keepdims=True) + 1e-06)


def softmax_rounded(scores):
    row_max = jnp.max(scores, axis=-1, keepdims=True)
    weights = jnp.exp(scores - row_max)
    return (weights / jnp.sum(weights, axis=-1, keepdims=True)).astype(jnp.bfloat16)


def pad_slots(values, slot_total):
    missing = slot_total - values.shape[1]
    filler = jnp.zeros((values.shape[0], missing, values.shape[2]), values.dtype)
    return jnp.concatenate([values, filler], axis=1)


def causal_block(queries, keys_all, values_all, span_rows, score_scale):
    total_rows = queries.shape[0]
    block_rows = min(512, total_rows)
    scores = (
        jnp.einsum("qsd,ksd->sqk", queries, keys_all, preferred_element_type=jnp.float32)
        * score_scale
    )
    allowed = (
        jnp.arange(0, block_rows)[:, None] // span_rows
        >= jnp.arange(block_rows)[None, :] // span_rows
    )
    scores = jnp.where(allowed[None], scores, -1e30)
    result = jnp.einsum(
        "sqk,ksd->qsd", softmax_rounded(scores), values_all, preferred_element_type=jnp.float32
    )
    pieces = result.astype(jnp.bfloat16)
    return pieces


def text_attend(queries, text_k, text_v, score_scale):
    scores = (
        jnp.einsum("qsd,tsd->sqt", queries, text_k, preferred_element_type=jnp.float32)
        * score_scale
    )
    return jnp.einsum(
        "sqt,tsd->qsd", softmax_rounded(scores), text_v, preferred_element_type=jnp.float32
    ).astype(jnp.bfloat16)


def per_device(
    hidden,
    incoming,
    levels,
    mod_table,
    query_weight,
    key_weight,
    value_weight,
    output_weight,
    query_gain,
    key_gain,
    text_keys,
    text_values,
):
    own_index = lax.axis_index("queue")
    queue_size = lax.axis_size("queue")
    span_rows, model_width = hidden.shape
    head_size = model_width // HEADS
    score_scale = 1.0 / math.sqrt(head_size)
    slot_total = -(-HEADS // queue_size) * queue_size
    own_level = lax.dynamic_index_in_dim(levels, own_index, 0, keepdims=False)
    modulation = lax.dynamic_index_in_dim(mod_table, own_level, 0, keepdims=False).astype(
        jnp.float32
    )
    stacked_weights = jnp.stack([query_weight, key_weight, value_weight])
    text_local = text_keys.shape[0]
    text_k_slots, text_v_slots = (
        lax.all_to_all(
            pad_slots(text_keys.reshape(text_local, HEADS, head_size), slot_total),
            "queue",
            split_axis=1,
            concat_axis=0,
            tiled=True,
        ),
        lax.all_to_all(
            pad_slots(text_values.reshape(text_local, HEADS, head_size), slot_total),
            "queue",
            split_axis=1,
            concat_axis=0,
            tiled=True,
        ),
    )
    queue_state = hidden
    for section_index in range(STEPS):
        shifted = passed_along(queue_state, "queue", 1)
        queue_state = jnp.where(own_index == 0, incoming[section_index], shifted)
        current = queue_state.astype(jnp.float32)
        modulated = (normalize(current) * (1.0 + modulation[1]) + modulation[0]).astype(
            jnp.bfloat16
        )
        columns = jnp.einsum(
            "rd,cdw->crw",
            lax.all_gather(modulated, "queue", axis=0, tiled=True),
            stacked_weights,
            preferred_element_type=jnp.float32,
        )
        own_rows = lax.all_to_all(
            columns.astype(jnp.bfloat16), "queue", split_axis=1, concat_axis=2, tiled=True
        ).astype(columns.dtype)
        query_heads = (
            (normalize(own_rows[0]) * query_gain)
            .astype(jnp.bfloat16)
            .reshape(span_rows, HEADS, head_size)
        )
        key_heads = (
            (normalize(own_rows[1]) * key_gain)
            .astype(jnp.bfloat16)
            .reshape(span_rows, HEADS, head_size)
        )
        value_heads = own_rows[2].astype(jnp.bfloat16).reshape(span_rows, HEADS, head_size)
        query_slots, key_slots, value_slots = (
            lax.all_to_all(
                pad_slots(query_heads, slot_total), "queue", split_axis=1, concat_axis=0, tiled=True
            ),
            lax.all_to_all(
                pad_slots(key_heads, slot_total), "queue", split_axis=1, concat_axis=0, tiled=True
            ),
            lax.all_to_all(
                pad_slots(value_heads, slot_total), "queue", split_axis=1, concat_axis=0, tiled=True
            ),
        )
        attended_slots = causal_block(query_slots, key_slots, value_slots, span_rows, score_scale)
        crossed_slots = text_attend(query_slots, text_k_slots, text_v_slots, score_scale)
        attended_back, crossed_back = (
            lax.all_to_all(attended_slots, "queue", split_axis=0, concat_axis=1, tiled=True),
            lax.all_to_all(crossed_slots, "queue", split_axis=0, concat_axis=1, tiled=True),
        )
        attended = attended_back[:, :HEADS]
        crossed = crossed_back[:, :HEADS]
        combined = (
            (attended.astype(jnp.float32) + crossed.astype(jnp.float32))
            .astype(jnp.bfloat16)
            .reshape(span_rows, model_width)
        )
        out_columns = jnp.dot(
            lax.all_gather(combined, "queue", axis=0, tiled=True),
            output_weight,
            preferred_element_type=jnp.float32,
        )
        projected = lax.all_to_all(
            out_columns.astype(jnp.bfloat16), "queue", split_axis=0, concat_axis=1, tiled=True
        ).astype(out_columns.dtype)
        queue_state = (current + modulation[2] * projected).astype(jnp.bfloat16)
    return queue_state


def solution(mesh):
    in_specs = (
        P(("groups", "queue"), None),
        P(None, "groups", None),
        P(),
        P(),
        P(None, "queue"),
        P(None, "queue"),
        P(None, "queue"),
        P(None, "queue"),
        P(),
        P(),
        P(("groups", "queue"), None),
        P(("groups", "queue"), None),
    )
    out_specs = P(("groups", "queue"), None)
    return jax.shard_map(
        per_device, mesh=mesh, in_specs=in_specs, out_specs=out_specs, check_vma=False
    )
```

profile of v0, /device:TPU:0, one launch (start us, length us, event | category | flops | bytes accessed | tf_op | source)
XLA Modules:
  0.0 410.4 jit_solution(12436979856965290002)
XLA Ops:
  6.5 2.7 collective-permute-start
  9.2 1.2 dynamic_slice.8
  14.0 1.1 fusion.34
  17.7 7.2 %all-to-all-start.6 = ((bf16[32,48,128]{2,0,1:T(8,128)(2,1)}), bf16[32,48,128]{2,0,1:T(8,128)(2,1)}, u32[]{:S(2)}, u32[]{:S(2)}) async-start(bf16[32,48,128]{2,0,1:T(8,128)(2,1)} %concatenate.28.clone), calls=%async_computation.6 | async-start | bytes 786432 | tf_op jit(solution)/shard_map/all_to_all | solution.py:90
  26.8 12.4 %all-to-all-done.6 = bf16[32,48,128]{2,0,1:T(8,128)(2,1)} async-done(((bf16[32,48,128]{2,0,1:T(8,128)(2,1)}), bf16[32,48,128]{2,0,1:T(8,128)(2,1)}, u32[]{:S(2)}, u32[]{:S(2)}) %all-to-all-start.6) | async-done | bytes 393248 | tf_op jit(solution)/shard_map/all_to_all | solution.py:90
  39.1 4.2 %all-to-all-start.5 = ((bf16[32,48,128]{2,0,1:T(8,128)(2,1)}), bf16[32,48,128]{2,0,1:T(8,128)(2,1)}, u32[]{:S(2)}, u32[]{:S(2)}) async-start(bf16[32,48,128]{2,0,1:T(8,128)(2,1)} %concatenate.27.clone), calls=%async_computation.5 | async-start | bytes 786432 | tf_op jit(solution)/shard_map/all_to_all | solution.py:97
  43.3 18.6 %all-gather.5.cloned.1.call-done = bf16[128,5120]{1,0:T(8,128)(2,1)} async-done(((bf16[8,5120]{1,0:T(8,128)(2,1)}), bf16[128,5120]{1,0:T(8,128)(2,1)}) %all-gather.5.cloned.1.call-update) | async-done | bytes 1310736 | tf_op jit(solution)/shard_map/all_gather | solution.py:115
  62.0 7.3 %fusion.23 = bf16[3,128,320]{1,2,0:T(8,128)(2,1)} fusion(bf16[128,5120]{1,0:T(8,128)(2,1)} %all-gather.5.cloned.1.call-done, bf16[1,5120,320]{1,2,0:T(8,128)(2,1)} %bitcast.210, bf16[1,5120,320]{1,2,0:T(8,128)(2,1)} %bitcast.212, bf16[1,5120,320]{1,2,0:T(8,128)(2,1)} %bitcast.214), kind=kOutput, calls=%fused_computation.20 | convolution fusion | flops 1268244480 | bytes 11386880 | tf_op jit(solution)/shard_map/rd,cdw->crw/dot_general | solution.py:113
  69.3 1.9 copy.99
  71.2 4.2 %all-to-all-start = ((bf16[3,128,320]{2,0,1:T(4,128)(2,1)}), bf16[3,128,320]{2,0,1:T(4,128)(2,1)}, u32[]{:S(2)}, u32[]{:S(2)}) async-start(bf16[3,128,320]{2,0,1:T(4,128)(2,1)} %copy.99), calls=%async_computation | async-start | bytes 786432 | tf_op jit(solution)/shard_map/all_to_all | solution.py:119
  76.1 1.8 copy.118
  77.9 1.8 copy.116
  79.7 7.9 %all-to-all-done = bf16[3,128,320]{2,0,1:T(4,128)(2,1)} async-done(((bf16[3,128,320]{2,0,1:T(4,128)(2,1)}), bf16[3,128,320]{2,0,1:T(4,128)(2,1)}, u32[]{:S(2)}, u32[]{:S(2)}) %all-to-all-start) | async-done | bytes 245792 | tf_op jit(solution)/shard_map/all_to_all | solution.py:119
  87.6 1.1 fusion.77
  94.9 4.2 %all-to-all-start.2 = ((bf16[8,48,128]{2,0,1:T(8,128)(2,1)}), bf16[8,48,128]{2,0,1:T(8,128)(2,1)}, u32[]{:S(2)}, u32[]{:S(2)}) async-start(bf16[8,48,128]{2,0,1:T(8,128)(2,1)} %concatenate.25.clone), calls=%async_computation.2 | async-start | bytes 196608 | tf_op jit(solution)/shard_map/all_to_all | solution.py:134
  102.5 4.0 all-to-all-done.2
  106.5 3.5 all-to-all-start.3
  110.0 2.2 convolution_multiply_fusion.1
  112.2 5.1 %all-to-all-done.3 = bf16[8,48,128]{2,0,1:T(8,128)(2,1)S(1)} async-done(((bf16[8,48,128]{2,0,1:T(8,128)(2,1)}), bf16[8,48,128]{2,0,1:T(8,128)(2,1)S(1)}, u32[]{:S(2)}, u32[]{:S(2)}) %all-to-all-start.3) | async-done | bytes 98336 | tf_op jit(solution)/shard_map/all_to_all | solution.py:137
  117.3 4.2 %all-to-all-start.1 = ((bf16[8,48,128]{2,0,1:T(8,128)(2,1)}), bf16[8,48,128]{2,0,1:T(8,128)(2,1)}, u32[]{:S(2)}, u32[]{:S(2)}) async-start(bf16[8,48,128]{2,0,1:T(8,128)(2,1)} %concatenate.24.clone), calls=%async_computation.1 | async-start | bytes 196608 | tf_op jit(solution)/shard_map/all_to_all | solution.py:140
  121.5 1.1 fusion.27
  123.3 2.1 fusion.81
  125.4 3.5 all-to-all-done.1
  128.9 1.8 fusion.30
  130.6 1.7 copy.112
  132.3 3.5 all-to-all-start.4
  135.8 3.1 fusion.32
  138.9 1.7 copy.120
  140.6 3.1 all-to-all-done.4
  143.7 4.2 %all-to-all-start.7 = ((bf16[128,3,128]{2,1,0:T(4,128)(2,1)}), bf16[128,3,128]{2,1,0:T(4,128)(2,1)}, u32[]{:S(2)}, u32[]{:S(2)}) async-start(bf16[128,3,128]{2,1,0:T(4,128)(2,1)} %copy.120), calls=%async_computation.7 | async-start | bytes 262144 | tf_op jit(solution)/shard_map/all_to_all | solution.py:148
  148.0 7.8 %all-to-all-done.7 = bf16[128,3,128]{2,1,0:T(4,128)(2,1)} async-done(((bf16[128,3,128]{2,1,0:T(4,128)(2,1)}), bf16[128,3,128]{2,1,0:T(4,128)(2,1)}, u32[]{:S(2)}, u32[]{:S(2)}) %all-to-all-start.7) | async-done | bytes 98336 | tf_op jit(solution)/shard_map/all_to_all | solution.py:148
  157.5 36.5 %all-gather.7.cloned.1.call-done = bf16[128,5120]{1,0:T(8,128)(2,1)} async-done(((bf16[8,5120]{1,0:T(8,128)(2,1)}), bf16[128,5120]{1,0:T(8,128)(2,1)}) %all-gather.7.cloned.1.call-update) | async-done | bytes 1310736 | tf_op jit(solution)/shard_map/all_gather | solution.py:158
  193.9 2.3 convolution_convert_fusion.5
  196.4 10.7 %all_to_all.260 = bf16[16,8,320]{2,1,0:T(8,128)(2,1)S(1)} all-to-all(bf16[16,8,320]{2,1,0:T(8,128)(2,1)S(1)} %bitcast.192), channel_id=1, replica_groups=mesh['groups'=2,'queue'=16] {'queue'}, dimensions={0} | all-to-all | bytes 163840 | tf_op jit(solution)/shard_map/all_to_all | solution.py:162
  208.8 1.3 collective-permute-start.1
  211.0 1.0 fusion.39
  212.1 1.5 fusion.42
  213.6 40.5 %all-gather.9.cloned.1.call-done = bf16[128,5120]{1,0:T(8,128)(2,1)} async-done(((bf16[8,5120]{1,0:T(8,128)(2,1)}), bf16[128,5120]{1,0:T(8,128)(2,1)}) %all-gather.9.cloned.1.call-update) | async-done | bytes 1310736 | tf_op jit(solution)/shard_map/all_gather | solution.py:115
  254.1 7.3 %fusion.20 = bf16[3,128,320]{1,2,0:T(8,128)(2,1)} fusion(bf16[128,5120]{1,0:T(8,128)(2,1)} %all-gather.9.cloned.1.call-done, bf16[1,5120,320]{1,2,0:T(8,128)(2,1)} %bitcast.211, bf16[1,5120,320]{1,2,0:T(8,128)(2,1)} %bitcast.213, bf16[1,5120,320]{1,2,0:T(8,128)(2,1)} %bitcast.215), kind=kOutput, calls=%fused_computation.19 | convolution fusion | flops 1268244480 | bytes 11386880 | tf_op jit(solution)/shard_map/rd,cdw->crw/dot_general | solution.py:113
  261.4 1.9 copy.125
  263.3 15.7 %all_to_all.261 = bf16[3,128,320]{2,0,1:T(4,128)(2,1)S(1)} all-to-all(bf16[3,128,320]{2,0,1:T(4,128)(2,1)} %copy.125), channel_id=1, replica_groups=mesh['groups'=2,'queue'=16] {'queue'}, dimensions={1} | all-to-all | bytes 491520 | tf_op jit(solution)/shard_map/all_to_all | solution.py:119
  281.7 1.7 convert_element_type.191
  284.9 1.6 copy.133
  286.6 1.7 squeeze.34
  289.0 1.0 squeeze.33
  291.5 3.5 all-to-all-start.11
  296.7 5.7 %all-to-all-done.11 = bf16[8,48,128]{2,0,1:T(8,128)(2,1)S(1)} async-done(((bf16[8,48,128]{2,0,1:T(8,128)(2,1)}), bf16[8,48,128]{2,0,1:T(8,128)(2,1)S(1)}, u32[]{:S(2)}, u32[]{:S(2)}) %all-to-all-start.11) | async-done | bytes 98336 | tf_op jit(solution)/shard_map/all_to_all | solution.py:134
  302.4 3.5 all-to-all-start.12
  305.9 2.1 convolution_multiply_fusion
  308.0 5.2 %all-to-all-done.12 = bf16[8,48,128]{2,0,1:T(8,128)(2,1)S(1)} async-done(((bf16[8,48,128]{2,0,1:T(8,128)(2,1)}), bf16[8,48,128]{2,0,1:T(8,128)(2,1)S(1)}, u32[]{:S(2)}, u32[]{:S(2)}) %all-to-all-start.12) | async-done | bytes 98336 | tf_op jit(solution)/shard_map/all_to_all | solution.py:137
  313.2 4.3 %all-to-all-start.10 = ((bf16[8,48,128]{2,0,1:T(8,128)(2,1)}), bf16[8,48,128]{2,0,1:T(8,128)(2,1)}, u32[]{:S(2)}, u32[]{:S(2)}) async-start(bf16[8,48,128]{2,0,1:T(8,128)(2,1)} %concatenate.29.clone), calls=%async_computation.10 | async-start | bytes 196608 | tf_op jit(solution)/shard_map/all_to_all | solution.py:140
  319.2 1.5 fusion.85
  320.7 4.1 all-to-all-done.10
  324.8 1.3 fusion.31
  326.8 3.5 all-to-all-start.13
  330.4 3.1 fusion.33
  333.5 1.7 copy.142
  335.1 3.1 all-to-all-done.13
  338.2 4.2 %all-to-all-start.14 = ((bf16[128,3,128]{2,1,0:T(4,128)(2,1)}), bf16[128,3,128]{2,1,0:T(4,128)(2,1)}, u32[]{:S(2)}, u32[]{:S(2)}) async-start(bf16[128,3,128]{2,1,0:T(4,128)(2,1)} %copy.142), calls=%async_computation.14 | async-start | bytes 262144 | tf_op jit(solution)/shard_map/all_to_all | solution.py:148
  342.5 7.8 %all-to-all-done.14 = bf16[128,3,128]{2,1,0:T(4,128)(2,1)} async-done(((bf16[128,3,128]{2,1,0:T(4,128)(2,1)}), bf16[128,3,128]{2,1,0:T(4,128)(2,1)}, u32[]{:S(2)}, u32[]{:S(2)}) %all-to-all-start.14) | async-done | bytes 98336 | tf_op jit(solution)/shard_map/all_to_all | solution.py:148
  352.0 36.4 %all-gather.11.cloned.1.call-done = bf16[128,5120]{1,0:T(8,128)(2,1)} async-done(((bf16[8,5120]{1,0:T(8,128)(2,1)}), bf16[128,5120]{1,0:T(8,128)(2,1)}) %all-gather.11.cloned.1.call-update) | async-done | bytes 1310736 | tf_op jit(solution)/shard_map/all_gather | solution.py:158
  388.4 2.3 convolution_convert_fusion.4
  390.9 10.7 %all_to_all.262 = bf16[16,8,320]{2,1,0:T(8,128)(2,1)S(1)} all-to-all(bf16[16,8,320]{2,1,0:T(8,128)(2,1)S(1)} %bitcast.193), channel_id=1, replica_groups=mesh['groups'=2,'queue'=16] {'queue'}, dimensions={0} | all-to-all | bytes 163840 | tf_op jit(solution)/shard_map/all_to_all | solution.py:162
  402.3 1.6 fusion.43
  (89 shorter events, 34.8 us)
Async XLA Ops:
  6.5 187.4 %copy-start = (bf16[5120,320]{0,1:T(8,128)(2,1)S(1)}, bf16[5120,320]{0,1:T(8,128)(2,1)}, u32[]{:S(2)}) copy-start(bf16[5120,320]{0,1:T(8,128)(2,1)} %param.19) | copy-start | bytes 9830404
  6.5 55.4 %all-gather.5.cloned.1.call-start = ((), (), s32[]{:S(2)}) async-start(), calls=%async_computation.16 | async-start | bytes 1392640 | tf_op jit(solution)/shard_map/all_gather | solution.py:115
  6.5 7.5 %collective-permute-start = (bf16[8,5120]{1,0:T(8,128)(2,1)}, bf16[8,5120]{1,0:T(8,128)(2,1)S(1)}, u32[]{:S(2)}, u32[]{:S(2)}) collective-permute-start(bf16[8,5120]{1,0:T(8,128)(2,1)} %param.12), channel_id=1, source_target_pairs={{0,1},{1,2},{2,3},{3,4},{4,5},{5,6},{6,7},{7,8},{8,9},{9,10},{10,1... | collective-permute-start | bytes 245768 | tf_op jit(solution)/shard_map/ppermute | solution.py:15
  14.0 55.3 %copy-start.2 = (f32[1,1,5120]{2,0,1:T(1,128)}, f32[1,1,5120]{2,0,1:T(1,128)S(1)}, u32[]{:S(2)}) copy-start(f32[1,1,5120]{2,0,1:T(1,128)S(1)} %get-tuple-element.22) | copy-start | bytes 61444
  14.0 55.3 %copy-start.3 = (f32[1,1,5120]{2,0,1:T(1,128)}, f32[1,1,5120]{2,0,1:T(1,128)S(1)}, u32[]{:S(2)}) copy-start(f32[1,1,5120]{2,0,1:T(1,128)S(1)} %get-tuple-element.23) | copy-start | bytes 61444
  17.7 21.5 %all-to-all-start.6 = ((bf16[32,48,128]{2,0,1:T(8,128)(2,1)}), bf16[32,48,128]{2,0,1:T(8,128)(2,1)}, u32[]{:S(2)}, u32[]{:S(2)}) async-start(bf16[32,48,128]{2,0,1:T(8,128)(2,1)} %concatenate.28.clone), calls=%async_computation.6 | async-start | bytes 786432 | tf_op jit(solution)/shard_map/all_to_all | solution.py:90
  39.1 32.0 %all-to-all-start.5 = ((bf16[32,48,128]{2,0,1:T(8,128)(2,1)}), bf16[32,48,128]{2,0,1:T(8,128)(2,1)}, u32[]{:S(2)}, u32[]{:S(2)}) async-start(bf16[32,48,128]{2,0,1:T(8,128)(2,1)} %concatenate.27.clone), calls=%async_computation.5 | async-start | bytes 786432 | tf_op jit(solution)/shard_map/all_to_all | solution.py:97
  71.2 16.4 %all-to-all-start = ((bf16[3,128,320]{2,0,1:T(4,128)(2,1)}), bf16[3,128,320]{2,0,1:T(4,128)(2,1)}, u32[]{:S(2)}, u32[]{:S(2)}) async-start(bf16[3,128,320]{2,0,1:T(4,128)(2,1)} %copy.99), calls=%async_computation | async-start | bytes 786432 | tf_op jit(solution)/shard_map/all_to_all | solution.py:119
  94.9 11.6 %all-to-all-start.2 = ((bf16[8,48,128]{2,0,1:T(8,128)(2,1)}), bf16[8,48,128]{2,0,1:T(8,128)(2,1)}, u32[]{:S(2)}, u32[]{:S(2)}) async-start(bf16[8,48,128]{2,0,1:T(8,128)(2,1)} %concatenate.25.clone), calls=%async_computation.2 | async-start | bytes 196608 | tf_op jit(solution)/shard_map/all_to_all | solution.py:134
  106.5 10.9 %all-to-all-start.3 = ((bf16[8,48,128]{2,0,1:T(8,128)(2,1)}), bf16[8,48,128]{2,0,1:T(8,128)(2,1)S(1)}, u32[]{:S(2)}, u32[]{:S(2)}) async-start(bf16[8,48,128]{2,0,1:T(8,128)(2,1)} %concatenate.26.clone), calls=%async_computation.3 | async-start | bytes 196608 | tf_op jit(solution)/shard_map/all_to_all | solution.py:137
  117.3 4.2 %copy-start.4 = (bf16[8,48,128]{2,0,1:T(8,128)(2,1)}, bf16[8,48,128]{2,0,1:T(8,128)(2,1)S(1)}, u32[]{:S(2)}) copy-start(bf16[8,48,128]{2,0,1:T(8,128)(2,1)S(1)} %all-to-all-done.3) | copy-start | bytes 294916
  117.3 11.6 %all-to-all-start.1 = ((bf16[8,48,128]{2,0,1:T(8,128)(2,1)}), bf16[8,48,128]{2,0,1:T(8,128)(2,1)}, u32[]{:S(2)}, u32[]{:S(2)}) async-start(bf16[8,48,128]{2,0,1:T(8,128)(2,1)} %concatenate.24.clone), calls=%async_computation.1 | async-start | bytes 196608 | tf_op jit(solution)/shard_map/all_to_all | solution.py:140
  132.3 11.4 %all-to-all-start.4 = ((bf16[128,3,128]{2,1,0:T(4,128)(2,1)}), bf16[128,3,128]{2,1,0:T(4,128)(2,1)S(1)}, u32[]{:S(2)}, u32[]{:S(2)}) async-start(bf16[128,3,128]{2,1,0:T(4,128)(2,1)} %copy.112), calls=%async_computation.4 | async-start | bytes 262144 | tf_op jit(solution)/shard_map/all_to_all | solution.py:147
  143.7 12.1 %all-to-all-start.7 = ((bf16[128,3,128]{2,1,0:T(4,128)(2,1)}), bf16[128,3,128]{2,1,0:T(4,128)(2,1)}, u32[]{:S(2)}, u32[]{:S(2)}) async-start(bf16[128,3,128]{2,1,0:T(4,128)(2,1)} %copy.120), calls=%async_computation.7 | async-start | bytes 262144 | tf_op jit(solution)/shard_map/all_to_all | solution.py:148
  147.9 46.1 %all-gather.7.cloned.1.call-start = ((), (), s32[]{:S(2)}) async-start(), calls=%async_computation.17 | async-start | bytes 1392640 | tf_op jit(solution)/shard_map/all_gather | solution.py:158
  157.4 96.7 %all-gather.9.cloned.1.call-start = ((), (), s32[]{:S(2)}) async-start(), calls=%async_computation.18 | async-start | bytes 1392640 | tf_op jit(solution)/shard_map/all_gather | solution.py:115
  208.8 2.2 collective-permute-start.1
  291.5 10.9 %all-to-all-start.11 = ((bf16[8,48,128]{2,0,1:T(8,128)(2,1)}), bf16[8,48,128]{2,0,1:T(8,128)(2,1)S(1)}, u32[]{:S(2)}, u32[]{:S(2)}) async-start(bf16[8,48,128]{2,0,1:T(8,128)(2,1)} %concatenate.30.clone), calls=%async_computation.11 | async-start | bytes 196608 | tf_op jit(solution)/shard_map/all_to_all | solution.py:134
  302.4 10.9 %all-to-all-start.12 = ((bf16[8,48,128]{2,0,1:T(8,128)(2,1)}), bf16[8,48,128]{2,0,1:T(8,128)(2,1)S(1)}, u32[]{:S(2)}, u32[]{:S(2)}) async-start(bf16[8,48,128]{2,0,1:T(8,128)(2,1)} %concatenate.31.clone), calls=%async_computation.12 | async-start | bytes 196608 | tf_op jit(solution)/shard_map/all_to_all | solution.py:137
  313.2 11.6 %all-to-all-start.10 = ((bf16[8,48,128]{2,0,1:T(8,128)(2,1)}), bf16[8,48,128]{2,0,1:T(8,128)(2,1)}, u32[]{:S(2)}, u32[]{:S(2)}) async-start(bf16[8,48,128]{2,0,1:T(8,128)(2,1)} %concatenate.29.clone), calls=%async_computation.10 | async-start | bytes 196608 | tf_op jit(solution)/shard_map/all_to_all | solution.py:140
  318.5 0.7 copy-start.1
  326.8 11.4 %all-to-all-start.13 = ((bf16[128,3,128]{2,1,0:T(4,128)(2,1)}), bf16[128,3,128]{2,1,0:T(4,128)(2,1)S(1)}, u32[]{:S(2)}, u32[]{:S(2)}) async-start(bf16[128,3,128]{2,1,0:T(4,128)(2,1)} %copy.138), calls=%async_computation.13 | async-start | bytes 262144 | tf_op jit(solution)/shard_map/all_to_all | solution.py:147
  338.2 12.1 %all-to-all-start.14 = ((bf16[128,3,128]{2,1,0:T(4,128)(2,1)}), bf16[128,3,128]{2,1,0:T(4,128)(2,1)}, u32[]{:S(2)}, u32[]{:S(2)}) async-start(bf16[128,3,128]{2,1,0:T(4,128)(2,1)} %copy.142), calls=%async_computation.14 | async-start | bytes 262144 | tf_op jit(solution)/shard_map/all_to_all | solution.py:148
  342.4 46.0 %all-gather.11.cloned.1.call-start = ((), (), s32[]{:S(2)}) async-start(), calls=%async_computation.19 | async-start | bytes 1392640 | tf_op jit(solution)/shard_map/all_gather | solution.py:158
Sparse Core Ops, SparseCore 0:
  16.0 45.9 all-gather.4
  157.5 36.3 all-gather.6
  213.7 40.3 all-gather.8
  352.1 36.2 all-gather.10
where the time goes:
time: 413 us; the launch traced here: 410 us
  waiting for transfers between devices  203 us (49%)
  starting transfers between devices  58.3 us (14%)
  local copies, waits for them, and re-layouts  39.1 us (9%)
  matrix products  38.4 us (9%)
  blocking collectives  37 us (9%)
  other arithmetic  19.5 us (5%)
  between operations  15.5 us (4%)
    all_gather x2, waiting for transfers between devices, per_device(): lax.all_gather(combined, 'queue', axis=0, tiled=True)  72.9 us
    all_gather x2, waiting for transfers between devices, per_device(): lax.all_gather(modulated, 'queue', axis=0, tiled=True)  59.1 us
    all_to_all x2, blocking collectives, per_device(): lax.all_to_all(out_columns.astype(jnp.bfloat16), 'queue', split_axis=0, c...  21.3 us
    all_to_all x1, blocking collectives, per_device(): lax.all_to_all(columns.astype(jnp.bfloat16), 'queue', split_axis=1, conca...  15.7 us
    all_to_all x2, waiting for transfers between devices, per_device(): lax.all_to_all(crossed_slots, 'queue', split_axis=0, concat_axis=1, tiled...  15.6 us
    dot_general x2, matrix products, per_device(): jnp.einsum('rd,cdw->crw', lax.all_gather(modulated, 'queue', axis=0, tile...  14.6 us
    all_to_all x1, waiting for transfers between devices, per_device(): lax.all_to_all(pad_slots(text_keys.reshape(text_local, HEADS, head_size),...  12.4 us
    all_to_all x2, waiting for transfers between devices, per_device(): lax.all_to_all(pad_slots(key_heads, slot_total), 'queue', split_axis=1, c...  10.4 us
  transfers between devices with their start and end apart: 19, of which 17 were waited for; matrix products, arithmetic and copies ran while one was open for 11% of the time, Pallas kernels for 0%

commit v1 on v0

--- a/solution.py
+++ b/solution.py
@@ -1,8 +1,11 @@
+import functools
 import math
 
 import jax
 import jax.numpy as jnp
 from jax import lax
+from jax.experimental import pallas as pl
+from jax.experimental.pallas import tpu as pltpu
 from jax.sharding import PartitionSpec as P
 
 HEADS = 40
@@ -166,6 +169,466 @@
     return queue_state
 
 
+def dot_nt(a, b):
+    return lax.dot_general(a, b, (((1,), (1,)), ((), ())), preferred_element_type=jnp.float32)
+
+
+def fused_kernel(
+    n,
+    cols,
+    hidden,
+    incoming,
+    mods,
+    wq_hbm,
+    wk_hbm,
+    wv_hbm,
+    wo_hbm,
+    q_gain,
+    k_gain,
+    tkeys,
+    tvals,
+    out,
+    wq,
+    wk,
+    wv,
+    wo,
+    first,
+    gathered,
+    current,
+    full,
+    placed,
+    qb,
+    kb,
+    vb,
+    xsend,
+    xrecv,
+    ssend,
+    srecv,
+    tk,
+    tv,
+    osend,
+    orecv,
+    load_sems,
+    gsend_sems,
+    grecv_sems,
+    ssend_sems,
+    srecv_sems,
+    xsend_sems,
+    xrecv_sems,
+    tsend_sems,
+    trecv_sems,
+    osend_sems,
+    orecv_sems,
+):
+    me = lax.axis_index("queue")
+    span, width = hidden.shape
+    head = width // HEADS
+    rows = n * span
+    pair = 2 * cols
+    local = placed.shape[1]
+    shared = 2 * local - pair
+    step_off = pair - local
+    core = lax.rem(me, 2)
+    sibling = me + 1 - 2 * core
+    across = me + 2 - 4 * lax.rem(me // 2, 2)
+    outer = n // 4
+    start_col = pl.multiple_of((me // 2) * pair + core * step_off, 128)
+    mid = pl.multiple_of((1 - core) * step_off, 128)
+    trows = tkeys.shape[0]
+    scale = 1.0 / math.sqrt(head)
+
+    loads = [
+        pltpu.make_async_copy(s, d, load_sems.at[i])
+        for i, (s, d) in enumerate(((wq_hbm, wq), (wk_hbm, wk), (wv_hbm, wv), (wo_hbm, wo)))
+    ]
+    own = pltpu.make_async_copy(hidden, first.at[me], load_sems.at[4])
+    own.start()
+    own_tk = pltpu.make_async_copy(
+        tkeys.at[:, pl.ds(start_col, local)], tk.at[pl.ds(me * trows, trows)], load_sems.at[5]
+    )
+    own_tv = pltpu.make_async_copy(
+        tvals.at[:, pl.ds(start_col, local)], tv.at[pl.ds(me * trows, trows)], load_sems.at[6]
+    )
+    for item in loads + [own_tk, own_tv]:
+        item.start()
+
+    barrier = pltpu.get_barrier_semaphore()
+    for k in range(1, n):
+        pl.semaphore_signal(
+            barrier,
+            inc=1,
+            device_id={"queue": lax.rem(me + k, n)},
+            device_id_type=pl.DeviceIdType.MESH,
+        )
+    pl.semaphore_wait(barrier, n - 1)
+
+    pending = []
+
+    def remote(src, dst, send, recv, target):
+        return pltpu.make_async_remote_copy(
+            src_ref=src,
+            dst_ref=dst,
+            send_sem=send,
+            recv_sem=recv,
+            device_id={"queue": target},
+            device_id_type=pl.DeviceIdType.MESH,
+        )
+
+    def gather(buf, phase):
+        count = [0]
+
+        def push(slot, target):
+            i = count[0]
+            count[0] += 1
+            c = remote(
+                buf.at[slot],
+                buf.at[slot],
+                gsend_sems.at[phase, i],
+                grecv_sems.at[phase, slot],
+                target,
+            )
+            c.start()
+            pending.append(c)
+
+        def arrived(slot):
+            remote(
+                buf.at[slot],
+                buf.at[slot],
+                gsend_sems.at[phase, 0],
+                grecv_sems.at[phase, slot],
+                sibling,
+            ).wait_recv()
+
+        order = sorted(range(1, outer), key=lambda d: min(d, outer - d))
+        for d in order:
+            push(me, lax.rem(me + 4 * d, n))
+        push(me, across)
+        push(me, sibling)
+        for d in order:
+            slot = lax.rem(me + n - 4 * d, n)
+            arrived(slot)
+            push(slot, across)
+            push(slot, sibling)
+        for d in [0] + order:
+            slot = lax.rem(across + n - 4 * d, n)
+            arrived(slot)
+            push(slot, sibling)
+        for d in [0] + order:
+            arrived(lax.rem(sibling + n - 4 * d, n))
+        for d in [0] + order:
+            base = me + 3 - 2 * lax.rem(me, 4)
+            arrived(lax.rem(base + n - 4 * d, n))
+
+    def drain():
+        for c in pending:
+            c.wait_send()
+        pending.clear()
+
+    lane = lax.broadcasted_iota(jnp.int32, (rows, local), 1)
+    shift = core * (local - cols)
+    mine = (lane >= shift) & (lane < shift + cols)
+
+    def place(value):
+        placed[:, :cols] = value
+        placed[:, cols:] = jnp.zeros((rows, local - cols), jnp.float32)
+        y = placed[...]
+        return jnp.where(mine, jnp.where(core == 1, pltpu.roll(y, local - cols, 1), y), 0.0)
+
+    def assemble(buf, dst, base, count):
+        for p in range(n // 2):
+            a = buf[2 * p, :count]
+            b = buf[2 * p + 1, :count]
+            at = p * pair
+            kept = pl.ds(base, count)
+            dst[kept, at : at + step_off] = a[:, :step_off].astype(dst.dtype)
+            dst[kept, at + step_off : at + local] = (
+                a[:, step_off:].astype(jnp.float32) + b[:, :shared].astype(jnp.float32)
+            ).astype(dst.dtype)
+            dst[kept, at + local : at + pair] = b[:, shared:].astype(dst.dtype)
+
+    def modulate():
+        def body(i, carry):
+            r0 = pl.multiple_of(i * 2 * span, 2 * span)
+            c = current[pl.ds(r0, 2 * span), :]
+            c = c * lax.rsqrt(jnp.mean(c * c, axis=-1, keepdims=True) + 1e-06)
+
+            def rows_of(kind):
+                return jnp.concatenate(
+                    [
+                        jnp.broadcast_to(mods[kind, pl.ds(2 * i + e, 1), :], (span, width))
+                        for e in range(2)
+                    ],
+                    axis=0,
+                )
+
+            full[pl.ds(r0, 2 * span), :] = (c * (1.0 + rows_of(1)) + rows_of(0)).astype(
+                jnp.bfloat16
+            )
+            return carry
+
+        lax.fori_loop(0, n // 2, body, 0)
+
+    qg = q_gain[:, pl.ds(start_col, local)]
+    kg = k_gain[:, pl.ds(start_col, local)]
+    ones = jnp.ones((8, local), jnp.float32)
+    allowed = (
+        lax.broadcasted_iota(jnp.int32, (rows, rows), 0) // span
+        >= lax.broadcasted_iota(jnp.int32, (rows, rows), 1) // span
+    )
+
+    own.wait()
+    gather(first, 0)
+    text = []
+    for k in range(1, n):
+        target = lax.rem(me + k, n)
+        col = pl.multiple_of((target // 2) * pair + lax.rem(target, 2) * step_off, 128)
+        for kind, (s, d) in enumerate(((tkeys, tk), (tvals, tv))):
+            c = remote(
+                s.at[:, pl.ds(col, local)],
+                d.at[pl.ds(me * trows, trows)],
+                tsend_sems.at[kind, k],
+                trecv_sems.at[kind, me],
+                target,
+            )
+            c.start()
+            text.append(c)
+
+    for step in range(STEPS):
+        current[0:span, :] = incoming[step].astype(jnp.float32)
+        if step == 0:
+            for s in range(1, n):
+                current[s * span : (s + 1) * span, :] = first[s - 1].astype(jnp.float32)
+        else:
+            assemble(gathered.at[2 * step - 1], current, span, rows - span)
+        modulate()
+        if step == 0:
+            loads[0].wait()
+            loads[1].wait()
+        m = full[...]
+        q = place(jnp.dot(m, wq[...], preferred_element_type=jnp.float32))
+        ssend[step, 0] = dot_nt(ones, q * q)
+        qb[...] = (q * qg).astype(jnp.bfloat16)
+        k_ = place(jnp.dot(m, wk[...], preferred_element_type=jnp.float32))
+        ssend[step, 1] = dot_nt(ones, k_ * k_)
+        kb[...] = (k_ * kg).astype(jnp.bfloat16)
+        for k in range(1, n):
+            c = remote(
+                ssend.at[step],
+                srecv.at[step, me],
+                ssend_sems.at[step, k],
+                srecv_sems.at[step, me],
+                lax.rem(me + k, n),
+            )
+            c.start()
+            pending.append(c)
+        srecv[step, me] = ssend[step]
+        xsend[step, 0] = qb[:, pl.ds(mid, shared)]
+        xsend[step, 1] = kb[:, pl.ds(mid, shared)]
+        swap = remote(
+            xsend.at[step], xrecv.at[step], xsend_sems.at[step], xrecv_sems.at[step], sibling
+        )
+        swap.start()
+        if step == 0:
+            loads[2].wait()
+        vb[...] = place(jnp.dot(m, wv[...], preferred_element_type=jnp.float32)).astype(
+            jnp.bfloat16
+        )
+        swap.wait()
+        qb[:, pl.ds(mid, shared)] = qb[:, pl.ds(mid, shared)] + xrecv[step, 0]
+        kb[:, pl.ds(mid, shared)] = kb[:, pl.ds(mid, shared)] + xrecv[step, 1]
+        for k in range(1, n):
+            src = lax.rem(me + k, n)
+            remote(
+                ssend.at[step],
+                srecv.at[step, src],
+                ssend_sems.at[step, k],
+                srecv_sems.at[step, src],
+                sibling,
+            ).wait_recv()
+        total = jnp.sum(srecv[step], axis=0)
+        inv = lax.rsqrt(total * (1.0 / width) + 1e-06)
+        q_col = jnp.transpose(jnp.broadcast_to(inv[0, 0:1], (128, rows)))[:, 0:1] * scale
+        k_row = inv[1, 0:1]
+        if step == 0:
+            own_tk.wait()
+            own_tv.wait()
+            for k in range(1, n):
+                src = lax.rem(me + k, n)
+                for kind, d in enumerate((tk, tv)):
+                    remote(
+                        d.at[pl.ds(src * trows, trows)],
+                        d.at[pl.ds(src * trows, trows)],
+                        tsend_sems.at[kind, k],
+                        trecv_sems.at[kind, src],
+                        sibling,
+                    ).wait_recv()
+        parts = []
+        for h in range(local // head):
+            at = slice(h * head, (h + 1) * head)
+            qh = qb[:, at]
+            s = dot_nt(qh, kb[:, at]) * q_col * k_row
+            s = jnp.where(allowed, s, -1e30)
+            w = jnp.exp(s - jnp.max(s, axis=-1, keepdims=True))
+            a = jnp.dot(
+                w.astype(jnp.bfloat16), vb[:, at], preferred_element_type=jnp.float32
+            ) / jnp.sum(w, axis=-1, keepdims=True)
+            t = dot_nt(qh, tk[:, at]) * q_col
+            w = jnp.exp(t - jnp.max(t, axis=-1, keepdims=True))
+            b = jnp.dot(
+                w.astype(jnp.bfloat16), tv[:, at], preferred_element_type=jnp.float32
+            ) / jnp.sum(w, axis=-1, keepdims=True)
+            parts.append(a + b)
+        combined = jnp.where(mine, jnp.concatenate(parts, axis=1), 0.0).astype(jnp.bfloat16)
+        gathered[2 * step, me] = combined
+        gather(gathered.at[2 * step], 2 * step + 1)
+        assemble(gathered.at[2 * step], full, 0, rows)
+        if step == 0:
+            loads[3].wait()
+        projected = place(jnp.dot(full[...], wo[...], preferred_element_type=jnp.float32))
+        for s in range(n):
+            placed[s * span : (s + 1) * span, :] = jnp.broadcast_to(
+                mods[2, s : s + 1, pl.ds(start_col, local)], (span, local)
+            )
+        state = jnp.where(
+            mine, current[:, pl.ds(start_col, local)] + placed[...] * projected, 0.0
+        )
+        if step < STEPS - 1:
+            gathered[2 * step + 1, me] = state.astype(jnp.bfloat16)
+            gather(gathered.at[2 * step + 1], 2 * step + 2)
+        else:
+            osend[...] = state.reshape(n, span, local).astype(jnp.bfloat16)
+            for k in range(1, n):
+                target = lax.rem(me + k, n)
+                c = remote(
+                    osend.at[target],
+                    orecv.at[me],
+                    osend_sems.at[k],
+                    orecv_sems.at[me],
+                    target,
+                )
+                c.start()
+                pending.append(c)
+            orecv[me] = osend[me]
+    for k in range(1, n):
+        src = lax.rem(me + k, n)
+        remote(
+            osend.at[src], orecv.at[src], osend_sems.at[k], orecv_sems.at[src], sibling
+        ).wait_recv()
+    assemble(orecv, out, 0, span)
+    for c in text:
+        c.wait_send()
+    drain()
+
+
+def per_device_fused(
+    hidden,
+    incoming,
+    levels,
+    mod_table,
+    query_weight,
+    key_weight,
+    value_weight,
+    output_weight,
+    query_gain,
+    key_gain,
+    text_keys,
+    text_values,
+):
+    n = lax.axis_size("queue")
+    span, width = hidden.shape
+    cols = query_weight.shape[1]
+    head = width // HEADS
+    local = -(-cols // head) * head
+    shared = 2 * local - 2 * cols
+    rows = n * span
+    text = n * text_keys.shape[0]
+    mods = jnp.take(mod_table, levels, axis=0).transpose(1, 0, 2).astype(jnp.float32)
+    vmem = pl.BlockSpec(memory_space=pltpu.VMEM)
+    anywhere = pl.BlockSpec(memory_space=pl.ANY)
+    dma = pltpu.SemaphoreType.DMA
+    bf16, f32 = jnp.bfloat16, jnp.float32
+    weight = pltpu.VMEM((width, cols), bf16)
+    return pl.pallas_call(
+        functools.partial(fused_kernel, n, cols),
+        out_shape=jax.ShapeDtypeStruct((span, width), hidden.dtype),
+        in_specs=[anywhere, vmem, vmem] + [anywhere] * 4 + [vmem] * 2 + [anywhere] * 2,
+        out_specs=vmem,
+        scratch_shapes=[
+            weight,
+            weight,
+            weight,
+            weight,
+            pltpu.VMEM((n, span, width), bf16),
+            pltpu.VMEM((2 * STEPS - 1, n, rows, local), bf16),
+            pltpu.VMEM((rows, width), f32),
+            pltpu.VMEM((rows, width), bf16),
+            pltpu.VMEM((rows, local), f32),
+            pltpu.VMEM((rows, local), bf16),
+            pltpu.VMEM((rows, local), bf16),
+            pltpu.VMEM((rows, local), bf16),
+            pltpu.VMEM((STEPS, 2, rows, shared), bf16),
+            pltpu.VMEM((STEPS, 2, rows, shared), bf16),
+            pltpu.VMEM((STEPS, 2, 8, rows), f32),
+            pltpu.VMEM((STEPS, n, 2, 8, rows), f32),
+            pltpu.VMEM((text, local), bf16),
+            pltpu.VMEM((text, local), bf16),
+            pltpu.VMEM((n, span, local), bf16),
+            pltpu.VMEM((n, span, local), bf16),
+            dma((7,)),
+            dma((2 * STEPS, n)),
+            dma((2 * STEPS, n)),
+            dma((STEPS, n)),
+            dma((STEPS, n)),
+            dma((STEPS,)),
+            dma((STEPS,)),
+            dma((2, n)),
+            dma((2, n)),
+            dma((n,)),
+            dma((n,)),
+        ],
+        compiler_params=pltpu.CompilerParams(
+            collective_id=0, has_side_effects=True, vmem_limit_bytes=60 * 1024 * 1024
+        ),
+    )(
+        hidden,
+        incoming,
+        mods,
+        query_weight,
+        key_weight,
+        value_weight,
+        output_weight,
+        query_gain.reshape(1, width),
+        key_gain.reshape(1, width),
+        text_keys,
+        text_values,
+    )
+
+
+def fits_fused(count, rows_total, width, groups):
+    head = width // HEADS
+    cols = width // count
+    span = rows_total // (count * groups)
+    return (
+        count % 4 == 0
+        and head == 128
+        and span == 8
+        and (2 * cols) % head == 0
+        and cols % head == head // 2
+        and cols > head
+        and count * span == 128
+    )
+
+
+def choose(mesh):
+    def run(hidden, incoming, levels, mod_table, *rest):
+        count = lax.axis_size("queue")
+        if fits_fused(count, hidden.shape[0] * count, hidden.shape[1], 1):
+            return per_device_fused(hidden, incoming, levels, mod_table, *rest)
+        return per_device(hidden, incoming, levels, mod_table, *rest)
+
+    return run
+
+
 def solution(mesh):
     in_specs = (
         P(("groups", "queue"), None),
@@ -183,5 +646,5 @@
     )
     out_specs = P(("groups", "queue"), None)
     return jax.shard_map(
-        per_device, mesh=mesh, in_specs=in_specs, out_specs=out_specs, check_vma=False
-    )
+        choose(mesh), mesh=mesh, in_specs=in_specs, out_specs=out_specs, check_vma=False
+    )

time: 413 us -> 140 us (0.34)
  waiting for transfers between devices: 203 us -> 0 us
  Pallas kernels: 0 us -> 109 us
  starting transfers between devices: 58.3 us -> 0 us
  matrix products: 38.4 us -> 0 us
  blocking collectives: 37 us -> 0 us
  other arithmetic: 19.5 us -> 2.7 us
  between operations: 15.5 us -> 0.02 us
  local copies, waits for them, and re-layouts: 39.1 us -> 27.1 us
    all_gather x4 -> x0, waiting for transfers between devices: 132 us -> none  [the longest x2 72.9 us: per_device(): lax.all_gather(combined, 'queue', axis=0, tiled=True)]
    pallas_call x0 -> x1, Pallas kernels: none -> 109 us  [per_device_fused(): pl.pallas_call(functools.partial(fused_kernel, n, cols), out_shape=jax.Sh...]
    all_to_all x13 -> x0, waiting for transfers between devices: 69.7 us -> none  [the longest x2 15.6 us: per_device(): lax.all_to_all(crossed_slots, 'queue', split_axis=0, concat_axis=1, tiled...]
    all_to_all x13 -> x0, starting transfers between devices: 54.2 us -> none  [the longest x2 8.48 us: per_device(): lax.all_to_all(pad_slots(value_heads, slot_total), 'queue', split_axis=1,...]
    all_to_all x3 -> x0, blocking collectives: 37 us -> none  [the longest x2 21.3 us: per_device(): lax.all_to_all(out_columns.astype(jnp.bfloat16), 'queue', split_axis=0, c...]
    dot_general x12 -> x0, matrix products: 34.9 us -> none  [the longest x2 14.6 us: per_device(): jnp.einsum('rd,cdw->crw', lax.all_gather(modulated, 'queue', axis=0, tile...]
    unnamed x18 -> x7, local copies, waits for them, and re-layouts: 3.72 us -> 25.1 us
    convert_element_type x14 -> x0, local copies, waits for them, and re-layouts: 13.2 us -> none  [the longest x2 3.77 us: per_device(): columns.astype(jnp.bfloat16)]
  transfers between devices with their start and end apart: 19 -> 0, of which waited for: 17 -> 0; matrix products, arithmetic and copies ran while one was open for 11% -> 0% of each run, Pallas kernels for 0% -> 0%
where the time goes in v1:
time: 140 us; the launch traced here: 139 us
  Pallas kernels  109 us (78%)
  local copies, waits for them, and re-layouts  27.1 us (19%)
  other arithmetic  2.7 us (2%)
    pallas_call x1, Pallas kernels, per_device_fused(): pl.pallas_call(functools.partial(fused_kernel, n, cols), out_shape=jax.Sh...  109 us
    unnamed x7, local copies, waits for them, and re-layouts  25.1 us

profile of v1, /device:TPU:0, one launch (start us, length us, event | category | flops | bytes accessed | tf_op | source)
XLA Modules:
  0.0 139.2 jit_solution(16560526330954743112)
XLA Ops:
  0.0 0.0 copy-start
  0.0 0.8 compare_and_fusion
  0.8 0.7 compare_select_fusion
  1.6 0.3 copy-done
  1.9 2.0 %gather_fusion = bf16[16,3,5120]{2,0,1:T(8,128)(2,1)S(1)} fusion(bf16[96,3,5120]{2,0,1:T(8,128)(2,1)S(1)} %copy-done, s32[1024]{0:T(1024)S(1)} %pad_clamp_fusion), kind=kCustom, calls=%fused_computation | custom fusion | bytes 983104 | tf_op jit(solution)/shard_map/jit(_take)/gather | solution.py:545
  3.8 1.1 convert_bitcast_fusion.mods
  5.0 5.8 %copy.17.wq_hbm = bf16[5120,320]{1,0:T(8,128)(2,1)} copy(bf16[5120,320]{0,1:T(8,128)(2,1)} %param.16) | data formatting | bytes 6553600 | tf_op args[4]
  10.8 5.8 %copy.18.wk_hbm = bf16[5120,320]{1,0:T(8,128)(2,1)} copy(bf16[5120,320]{0,1:T(8,128)(2,1)} %param.17) | data formatting | bytes 6553600 | tf_op args[5]
  16.6 5.8 %copy.19.wv_hbm = bf16[5120,320]{1,0:T(8,128)(2,1)} copy(bf16[5120,320]{0,1:T(8,128)(2,1)} %param.18) | data formatting | bytes 6553600 | tf_op args[6]
  22.4 5.8 %copy.20.wo_hbm = bf16[5120,320]{1,0:T(8,128)(2,1)} copy(bf16[5120,320]{0,1:T(8,128)(2,1)} %param.19) | data formatting | bytes 6553600 | tf_op args[7]
  28.3 109.4 %shard_map.118 = bf16[8,5120]{1,0:T(8,128)(2,1)} custom-call(bf16[8,5120]{1,0:T(8,128)(2,1)} %hidden.1, bf16[2,8,5120]{2,1,0:T(8,128)(2,1)} %incoming.1, f32[3,16,5120]{2,1,0:T(8,128)} %convert_bitcast_fusion.mods, bf16[5120,320]{1,0:T(8,128)(2,1)} %copy.17.wq_hbm, bf16[5120,320]{1,0:T(8,128)(2,1)} %copy.18.wk_hbm, bf16[5120,320]{1,0:T(8,128)(2,1)} %copy.19.wv_hbm, ...), custom_call_target="tpu_custom_call" | custom-call | tf_op jit(solution)/shard_map/pallas_call | solution.py:551
  137.7 1.5 %copy.22 = bf16[8,5120]{1,0:T(8,128)(2,1)} copy(bf16[8,5120]{1,0:T(8,128)(2,1)} %shard_map.118) | data formatting | bytes 163840
  (1 shorter events, 0.0 us)
Async XLA Ops:
  0.0 1.8 %copy-start = (bf16[96,3,5120]{2,0,1:T(8,128)(2,1)S(1)}, bf16[96,3,5120]{2,0,1:T(8,128)(2,1)}, u32[]{:S(2)}) copy-start(bf16[96,3,5120]{2,0,1:T(8,128)(2,1)} %param.15) | copy-start | bytes 8847364

commit v2 on v1

--- a/solution.py
+++ b/solution.py
@@ -10,6 +10,8 @@
 
 HEADS = 40
 STEPS = 2
+FIRST_CHUNKS = 2
+CHUNKS = 2
 
 
 def passed_along(value, axis, steps):
@@ -178,7 +180,8 @@
     cols,
     hidden,
     incoming,
-    mods,
+    levels,
+    table_hbm,
     wq_hbm,
     wk_hbm,
     wv_hbm,
@@ -188,6 +191,8 @@
     tkeys,
     tvals,
     out,
+    table,
+    mods,
     wq,
     wk,
     wv,
@@ -226,6 +231,7 @@
     rows = n * span
     pair = 2 * cols
     local = placed.shape[1]
+    blocks = gathered.shape[2]
     shared = 2 * local - pair
     step_off = pair - local
     core = lax.rem(me, 2)
@@ -243,6 +249,8 @@
     ]
     own = pltpu.make_async_copy(hidden, first.at[me], load_sems.at[4])
     own.start()
+    own_table = pltpu.make_async_copy(table_hbm, table, load_sems.at[7])
+    own_table.start()
     own_tk = pltpu.make_async_copy(
         tkeys.at[:, pl.ds(start_col, local)], tk.at[pl.ds(me * trows, trows)], load_sems.at[5]
     )
@@ -252,6 +260,7 @@
     for item in loads + [own_tk, own_tv]:
         item.start()
 
+    own.wait()
     barrier = pltpu.get_barrier_semaphore()
     for k in range(1, n):
         pl.semaphore_signal(
@@ -274,55 +283,149 @@
             device_id_type=pl.DeviceIdType.MESH,
         )
 
-    def gather(buf, phase):
-        count = [0]
-
-        def push(slot, target):
-            i = count[0]
-            count[0] += 1
-            c = remote(
-                buf.at[slot],
-                buf.at[slot],
-                gsend_sems.at[phase, i],
-                grecv_sems.at[phase, slot],
+    def gather(view, chunks, phase, between=None):
+        bank = phase % 2
+        plane = lax.rem(me, 4)
+        depth = me // 4
+
+        def copy(slot, ch, kind, target):
+            return remote(
+                view(slot, ch),
+                view(slot, ch),
+                gsend_sems.at[bank, kind, slot, ch],
+                grecv_sems.at[phase, slot, ch],
                 target,
             )
+
+        def push(slot, ch, kind, target):
+            copy(slot, ch, kind, target).start()
+
+        def arrived(slot, ch):
+            copy(slot, ch, 3, sibling).wait_recv()
+
+        def upward(slot, ch, act):
+            @pl.when(depth < outer - 1)
+            def _():
+                act(copy(slot, ch, 0, lax.rem(me + 4, n)))
+
+        def downward(slot, ch, act):
+            @pl.when(depth > 0)
+            def _():
+                act(copy(slot, ch, 1, lax.rem(me + n - 4, n)))
+
+        def start(c):
             c.start()
-            pending.append(c)
-
-        def arrived(slot):
-            remote(
-                buf.at[slot],
-                buf.at[slot],
-                gsend_sems.at[phase, 0],
-                grecv_sems.at[phase, slot],
-                sibling,
-            ).wait_recv()
-
-        order = sorted(range(1, outer), key=lambda d: min(d, outer - d))
-        for d in order:
-            push(me, lax.rem(me + 4 * d, n))
-        push(me, across)
-        push(me, sibling)
-        for d in order:
-            slot = lax.rem(me + n - 4 * d, n)
-            arrived(slot)
-            push(slot, across)
-            push(slot, sibling)
-        for d in [0] + order:
-            slot = lax.rem(across + n - 4 * d, n)
-            arrived(slot)
-            push(slot, sibling)
-        for d in [0] + order:
-            arrived(lax.rem(sibling + n - 4 * d, n))
-        for d in [0] + order:
-            base = me + 3 - 2 * lax.rem(me, 4)
-            arrived(lax.rem(base + n - 4 * d, n))
+
+        for ch in range(chunks):
+            upward(me, ch, start)
+            downward(me, ch, start)
+            push(me, ch, 2, across)
+            push(me, ch, 3, sibling)
+
+        def line(act_in, act_up, act_down, act_side):
+            for d in range(1, outer):
+                for ch in range(chunks):
+
+                    @pl.when(depth >= d)
+                    def _():
+                        slot = lax.rem(me + n - 4 * d, n)
+                        act_in(slot, ch)
+                        upward(slot, ch, act_up)
+                        act_side(slot, ch)
+
+                    @pl.when(depth < outer - d)
+                    def _():
+                        slot = lax.rem(me + 4 * d, n)
+                        act_in(slot, ch)
+                        downward(slot, ch, act_down)
+                        act_side(slot, ch)
+
+        def sides(slot, ch):
+            push(slot, ch, 2, across)
+            push(slot, ch, 3, sibling)
+
+        line(arrived, start, start, sides)
+        if between is not None:
+            between()
+
+        far = [0] + list(range(1, outer))
+        for d in far:
+            for ch in range(chunks):
+                slot = lax.rem(across + n - 4 * d, n)
+                arrived(slot, ch)
+                push(slot, ch, 3, sibling)
+        opposite = me + 3 - 2 * plane
+        for base in (sibling, opposite):
+            for d in far:
+                for ch in range(chunks):
+                    arrived(lax.rem(base + n - 4 * d, n), ch)
+
+        def sent(c):
+            c.wait_send()
+
+        def finish():
+            for ch in range(chunks):
+                upward(me, ch, sent)
+                downward(me, ch, sent)
+                copy(me, ch, 2, across).wait_send()
+                copy(me, ch, 3, sibling).wait_send()
+
+            def sides_sent(slot, ch):
+                copy(slot, ch, 2, across).wait_send()
+                copy(slot, ch, 3, sibling).wait_send()
+
+            line(lambda slot, ch: None, sent, sent, sides_sent)
+            for d in far:
+                for ch in range(chunks):
+                    copy(lax.rem(across + n - 4 * d, n), ch, 3, sibling).wait_send()
+
+        return finish
 
     def drain():
         for c in pending:
             c.wait_send()
         pending.clear()
+
+    def pack(value, dst):
+        placed[...] = value
+        dst[:rows, :] = placed[:, pl.ds(pl.multiple_of(core * shared, 128), step_off)].astype(
+            jnp.bfloat16
+        )
+        half = rows // 2
+        folded = placed[:half, pl.ds(mid, shared)] + pltpu.roll(
+            placed[half:, pl.ds(mid, shared)], shared // 2, 1
+        )
+        fold = half * shared // step_off
+        for e in range(step_off // shared):
+            dst[rows:, e * shared : (e + 1) * shared] = folded[
+                e * fold : (e + 1) * fold
+            ].astype(jnp.bfloat16)
+
+    low = lax.broadcasted_iota(jnp.int32, (rows // 2, shared), 1) < shared // 2
+
+    def unpack(buf, dst, base, count):
+        for p in range(n // 2):
+            a, b = buf.at[2 * p], buf.at[2 * p + 1]
+            at = p * pair
+            half = rows // 2
+            dst[pl.ds(base, count), at : at + step_off] = a[:count, :].astype(dst.dtype)
+            dst[pl.ds(base, count), at + local : at + pair] = b[:count, :].astype(dst.dtype)
+            fa, fb = (
+                jnp.concatenate(
+                    [
+                        r[rows:, e * shared : (e + 1) * shared].astype(jnp.float32)
+                        for e in range(step_off // shared)
+                    ],
+                    axis=0,
+                )
+                for r in (a, b)
+            )
+            at = at + step_off
+            dst[pl.ds(base, half), at : at + shared] = jnp.where(low, fa, fb).astype(dst.dtype)
+            rest = pltpu.roll(jnp.where(low, fb, fa), shared // 2, 1)
+            dst[pl.ds(base + half, count - half), at : at + shared] = rest[
+                : count - half
+            ].astype(dst.dtype)
 
     lane = lax.broadcasted_iota(jnp.int32, (rows, local), 1)
     shift = core * (local - cols)
@@ -376,22 +479,41 @@
         >= lax.broadcasted_iota(jnp.int32, (rows, rows), 1) // span
     )
 
-    own.wait()
-    gather(first, 0)
     text = []
-    for k in range(1, n):
-        target = lax.rem(me + k, n)
-        col = pl.multiple_of((target // 2) * pair + lax.rem(target, 2) * step_off, 128)
-        for kind, (s, d) in enumerate(((tkeys, tk), (tvals, tv))):
-            c = remote(
-                s.at[:, pl.ds(col, local)],
-                d.at[pl.ds(me * trows, trows)],
-                tsend_sems.at[kind, k],
-                trecv_sems.at[kind, me],
-                target,
-            )
-            c.start()
-            text.append(c)
+
+    def send_text():
+        for k in range(1, n):
+            target = lax.rem(me + k, n)
+            col = pl.multiple_of((target // 2) * pair + lax.rem(target, 2) * step_off, 128)
+            for kind, (s, d) in enumerate(((tkeys, tk), (tvals, tv))):
+                c = remote(
+                    s.at[:, pl.ds(col, local)],
+                    d.at[pl.ds(me * trows, trows)],
+                    tsend_sems.at[kind, k],
+                    trecv_sems.at[kind, me],
+                    target,
+                )
+                c.start()
+                text.append(c)
+
+    def prepare():
+        send_text()
+        own_table.wait()
+        picks = (
+            lax.broadcasted_iota(jnp.int32, (table.shape[1], n), 0) == levels[...]
+        ).astype(jnp.float32)
+        picks = jnp.transpose(picks).astype(jnp.bfloat16)
+        for kind in range(3):
+            mods[kind] = jnp.dot(picks, table[kind], preferred_element_type=jnp.float32)
+
+    part = width // FIRST_CHUNKS
+    finish = gather(
+        lambda slot, ch: first.at[slot, :, pl.ds(ch * part, part)], FIRST_CHUNKS, 0, prepare
+    )
+    piece = blocks // CHUNKS
+
+    def block_view(phase):
+        return lambda slot, ch: gathered.at[phase, slot, pl.ds(ch * piece, piece)]
 
     for step in range(STEPS):
         current[0:span, :] = incoming[step].astype(jnp.float32)
@@ -399,16 +521,16 @@
             for s in range(1, n):
                 current[s * span : (s + 1) * span, :] = first[s - 1].astype(jnp.float32)
         else:
-            assemble(gathered.at[2 * step - 1], current, span, rows - span)
+            unpack(gathered.at[2 * step - 1], current, span, rows - span)
         modulate()
         if step == 0:
             loads[0].wait()
             loads[1].wait()
         m = full[...]
-        q = place(jnp.dot(m, wq[...], preferred_element_type=jnp.float32))
+        q = place(dot_nt(m, wq[...]))
         ssend[step, 0] = dot_nt(ones, q * q)
         qb[...] = (q * qg).astype(jnp.bfloat16)
-        k_ = place(jnp.dot(m, wk[...], preferred_element_type=jnp.float32))
+        k_ = place(dot_nt(m, wk[...]))
         ssend[step, 1] = dot_nt(ones, k_ * k_)
         kb[...] = (k_ * kg).astype(jnp.bfloat16)
         for k in range(1, n):
@@ -430,7 +552,7 @@
         swap.start()
         if step == 0:
             loads[2].wait()
-        vb[...] = place(jnp.dot(m, wv[...], preferred_element_type=jnp.float32)).astype(
+        vb[...] = place(dot_nt(m, wv[...])).astype(
             jnp.bfloat16
         )
         swap.wait()
@@ -478,13 +600,15 @@
                 w.astype(jnp.bfloat16), tv[:, at], preferred_element_type=jnp.float32
             ) / jnp.sum(w, axis=-1, keepdims=True)
             parts.append(a + b)
-        combined = jnp.where(mine, jnp.concatenate(parts, axis=1), 0.0).astype(jnp.bfloat16)
-        gathered[2 * step, me] = combined
-        gather(gathered.at[2 * step], 2 * step + 1)
-        assemble(gathered.at[2 * step], full, 0, rows)
+        pack(
+            jnp.where(mine, jnp.concatenate(parts, axis=1), 0.0), gathered.at[2 * step, me]
+        )
+        finish()
+        finish = gather(block_view(2 * step), CHUNKS, 2 * step + 1)
+        unpack(gathered.at[2 * step], full, 0, rows)
         if step == 0:
             loads[3].wait()
-        projected = place(jnp.dot(full[...], wo[...], preferred_element_type=jnp.float32))
+        projected = place(dot_nt(full[...], wo[...]))
         for s in range(n):
             placed[s * span : (s + 1) * span, :] = jnp.broadcast_to(
                 mods[2, s : s + 1, pl.ds(start_col, local)], (span, local)
@@ -493,8 +617,9 @@
             mine, current[:, pl.ds(start_col, local)] + placed[...] * projected, 0.0
         )
         if step < STEPS - 1:
-            gathered[2 * step + 1, me] = state.astype(jnp.bfloat16)
-            gather(gathered.at[2 * step + 1], 2 * step + 2)
+            pack(state, gathered.at[2 * step + 1, me])
+            finish()
+            finish = gather(block_view(2 * step + 1), CHUNKS, 2 * step + 2)
         else:
             osend[...] = state.reshape(n, span, local).astype(jnp.bfloat16)
             for k in range(1, n):
@@ -517,6 +642,7 @@
     assemble(orecv, out, 0, span)
     for c in text:
         c.wait_send()
+    finish()
     drain()
 
 
@@ -540,26 +666,29 @@
     head = width // HEADS
     local = -(-cols // head) * head
     shared = 2 * local - 2 * cols
+    step_off = 2 * cols - local
     rows = n * span
     text = n * text_keys.shape[0]
-    mods = jnp.take(mod_table, levels, axis=0).transpose(1, 0, 2).astype(jnp.float32)
     vmem = pl.BlockSpec(memory_space=pltpu.VMEM)
     anywhere = pl.BlockSpec(memory_space=pl.ANY)
     dma = pltpu.SemaphoreType.DMA
     bf16, f32 = jnp.bfloat16, jnp.float32
-    weight = pltpu.VMEM((width, cols), bf16)
+    weight = pltpu.VMEM((cols, width), bf16)
+    most = max(FIRST_CHUNKS, CHUNKS)
     return pl.pallas_call(
         functools.partial(fused_kernel, n, cols),
         out_shape=jax.ShapeDtypeStruct((span, width), hidden.dtype),
-        in_specs=[anywhere, vmem, vmem] + [anywhere] * 4 + [vmem] * 2 + [anywhere] * 2,
+        in_specs=[anywhere, vmem, vmem] + [anywhere] * 5 + [vmem] * 2 + [anywhere] * 2,
         out_specs=vmem,
         scratch_shapes=[
+            pltpu.VMEM((3, mod_table.shape[0], width), bf16),
+            pltpu.VMEM((3, n, width), f32),
             weight,
             weight,
             weight,
             weight,
             pltpu.VMEM((n, span, width), bf16),
-            pltpu.VMEM((2 * STEPS - 1, n, rows, local), bf16),
+            pltpu.VMEM((2 * STEPS - 1, n, rows * cols // step_off, step_off), bf16),
             pltpu.VMEM((rows, width), f32),
             pltpu.VMEM((rows, width), bf16),
             pltpu.VMEM((rows, local), f32),
@@ -574,9 +703,9 @@
             pltpu.VMEM((text, local), bf16),
             pltpu.VMEM((n, span, local), bf16),
             pltpu.VMEM((n, span, local), bf16),
-            dma((7,)),
-            dma((2 * STEPS, n)),
-            dma((2 * STEPS, n)),
+            dma((8,)),
+            dma((2, 4, n, most)),
+            dma((2 * STEPS, n, most)),
             dma((STEPS, n)),
             dma((STEPS, n)),
             dma((STEPS,)),
@@ -592,11 +721,12 @@
     )(
         hidden,
         incoming,
-        mods,
-        query_weight,
-        key_weight,
-        value_weight,
-        output_weight,
+        levels.reshape(1, n),
+        mod_table.transpose(1, 0, 2),
+        query_weight.T,
+        key_weight.T,
+        value_weight.T,
+        output_weight.T,
         query_gain.reshape(1, width),
         key_gain.reshape(1, width),
         text_keys,

time: 140 us -> 106 us (0.76)
  local copies, waits for them, and re-layouts: 27.1 us -> 1.53 us
  Pallas kernels: 109 us -> 104 us
  other arithmetic: 2.7 us -> 0 us
    unnamed x7 -> x1, local copies, waits for them, and re-layouts: 25.1 us -> 1.53 us
    pallas_call x1, Pallas kernels: 109 us -> 104 us  [per_device_fused(): pl.pallas_call(functools.partial(fused_kernel, n, cols), out_shape=jax.Sh...]
    gather x1 -> x0, local copies, waits for them, and re-layouts: 1.97 us -> none  [per_device_fused(): jnp.take(mod_table, levels, axis=0).transpose(1, 0, 2).astype(jnp.float32)]
where the time goes in v2:
time: 106 us; the launch traced here: 105 us
  Pallas kernels  104 us (98%)
  local copies, waits for them, and re-layouts  1.53 us (1%)
    pallas_call x1, Pallas kernels, per_device_fused(): pl.pallas_call(functools.partial(fused_kernel, n, cols), out_shape=jax.Sh...  104 us

profile of v2, /device:TPU:0, one launch (start us, length us, event | category | flops | bytes accessed | tf_op | source)
XLA Modules:
  0.0 105.5 jit_solution(11473354755667470979)
XLA Ops:
  0.0 104.0 %shard_map.118 = bf16[8,5120]{1,0:T(8,128)(2,1)} custom-call(bf16[8,5120]{1,0:T(8,128)(2,1)} %hidden.1, bf16[2,8,5120]{2,1,0:T(8,128)(2,1)} %incoming.1, s32[1,16]{1,0:T(1,128)} %bitcast.15, bf16[3,96,5120]{2,1,0:T(8,128)(2,1)} %bitcast.12, bf16[320,5120]{1,0:T(8,128)(2,1)} %bitcast.8, bf16[320,5120]{1,0:T(8,128)(2,1)} %bitcast.9, ...), custom_call_target="tpu_custom_call" | custom-call | tf_op jit(solution)/shard_map/pallas_call | solution.py:678
  104.0 1.5 %copy.14 = bf16[8,5120]{1,0:T(8,128)(2,1)} copy(bf16[8,5120]{1,0:T(8,128)(2,1)} %shard_map.118) | data formatting | bytes 163840

commit v3 on v2

--- a/solution.py
+++ b/solution.py
@@ -322,7 +322,7 @@
             push(me, ch, 2, across)
             push(me, ch, 3, sibling)
 
-        def line(act_in, act_up, act_down, act_side):
+        def line(act_in, act_up, act_down, act_side, after=None):
             for d in range(1, outer):
                 for ch in range(chunks):
 
@@ -339,21 +339,37 @@
                         act_in(slot, ch)
                         downward(slot, ch, act_down)
                         act_side(slot, ch)
+                if after is not None:
+                    after(d - 1)
 
         def sides(slot, ch):
             push(slot, ch, 2, across)
             push(slot, ch, 3, sibling)
 
-        line(arrived, start, start, sides)
-        if between is not None:
-            between()
-
         far = [0] + list(range(1, outer))
-        for d in far:
+
+        def relay(slot, ch):
+            arrived(slot, ch)
+            push(slot, ch, 3, sibling)
+
+        def other_row(d):
+            if d == outer - 2 and between is not None:
+                between()
             for ch in range(chunks):
-                slot = lax.rem(across + n - 4 * d, n)
-                arrived(slot, ch)
-                push(slot, ch, 3, sibling)
+                if d == 0:
+                    relay(across, ch)
+                else:
+
+                    @pl.when(depth >= d)
+                    def _():
+                        relay(lax.rem(across + n - 4 * d, n), ch)
+
+                    @pl.when(depth < outer - d)
+                    def _():
+                        relay(lax.rem(across + 4 * d, n), ch)
+
+        line(arrived, start, start, sides, other_row)
+        other_row(outer - 1)
         opposite = me + 3 - 2 * plane
         for base in (sibling, opposite):
             for d in far:
@@ -528,10 +544,10 @@
             loads[1].wait()
         m = full[...]
         q = place(dot_nt(m, wq[...]))
-        ssend[step, 0] = dot_nt(ones, q * q)
+        ssend[step, 0:1] = dot_nt(ones, q * q)[0:1]
         qb[...] = (q * qg).astype(jnp.bfloat16)
         k_ = place(dot_nt(m, wk[...]))
-        ssend[step, 1] = dot_nt(ones, k_ * k_)
+        ssend[step, 1:2] = dot_nt(ones, k_ * k_)[0:1]
         kb[...] = (k_ * kg).astype(jnp.bfloat16)
         for k in range(1, n):
             c = remote(
@@ -569,8 +585,16 @@
             ).wait_recv()
         total = jnp.sum(srecv[step], axis=0)
         inv = lax.rsqrt(total * (1.0 / width) + 1e-06)
-        q_col = jnp.transpose(jnp.broadcast_to(inv[0, 0:1], (128, rows)))[:, 0:1] * scale
-        k_row = inv[1, 0:1]
+        q_col = jnp.transpose(jnp.broadcast_to(inv[0:1], (rows, rows)))[:, 0:1] * scale
+        k_row = inv[1:2]
+        for h in range(local // head):
+            at = slice(h * head, (h + 1) * head)
+            s = dot_nt(qb[:, at], kb[:, at]) * q_col * k_row
+            s = jnp.where(allowed, s, -1e30)
+            w = jnp.exp(s - jnp.max(s, axis=-1, keepdims=True))
+            placed[:, at] = jnp.dot(
+                w.astype(jnp.bfloat16), vb[:, at], preferred_element_type=jnp.float32
+            ) / jnp.sum(w, axis=-1, keepdims=True)
         if step == 0:
             own_tk.wait()
             own_tv.wait()
@@ -587,19 +611,12 @@
         parts = []
         for h in range(local // head):
             at = slice(h * head, (h + 1) * head)
-            qh = qb[:, at]
-            s = dot_nt(qh, kb[:, at]) * q_col * k_row
-            s = jnp.where(allowed, s, -1e30)
-            w = jnp.exp(s - jnp.max(s, axis=-1, keepdims=True))
-            a = jnp.dot(
-                w.astype(jnp.bfloat16), vb[:, at], preferred_element_type=jnp.float32
-            ) / jnp.sum(w, axis=-1, keepdims=True)
-            t = dot_nt(qh, tk[:, at]) * q_col
+            t = dot_nt(qb[:, at], tk[:, at]) * q_col
             w = jnp.exp(t - jnp.max(t, axis=-1, keepdims=True))
             b = jnp.dot(
                 w.astype(jnp.bfloat16), tv[:, at], preferred_element_type=jnp.float32
             ) / jnp.sum(w, axis=-1, keepdims=True)
-            parts.append(a + b)
+            parts.append(placed[:, at] + b)
         pack(
             jnp.where(mine, jnp.concatenate(parts, axis=1), 0.0), gathered.at[2 * step, me]
         )
@@ -697,8 +714,8 @@
             pltpu.VMEM((rows, local), bf16),
             pltpu.VMEM((STEPS, 2, rows, shared), bf16),
             pltpu.VMEM((STEPS, 2, rows, shared), bf16),
-            pltpu.VMEM((STEPS, 2, 8, rows), f32),
-            pltpu.VMEM((STEPS, n, 2, 8, rows), f32),
+            pltpu.VMEM((STEPS, 2, rows), f32),
+            pltpu.VMEM((STEPS, n, 2, rows), f32),
             pltpu.VMEM((text, local), bf16),
             pltpu.VMEM((text, local), bf16),
             pltpu.VMEM((n, span, local), bf16),

time: 106 us -> 104 us (0.981)
  Pallas kernels: 104 us -> 102 us
    pallas_call x1, Pallas kernels: 104 us -> 102 us  [per_device_fused(): pl.pallas_call(functools.partial(fused_kernel, n, cols), out_shape=jax.Sh...]
where the time goes in v3:
time: 104 us; the launch traced here: 103 us
  Pallas kernels  102 us (98%)
  local copies, waits for them, and re-layouts  1.53 us (1%)
    pallas_call x1, Pallas kernels, per_device_fused(): pl.pallas_call(functools.partial(fused_kernel, n, cols), out_shape=jax.Sh...  102 us

profile of v3, /device:TPU:0, one launch (start us, length us, event | category | flops | bytes accessed | tf_op | source)
XLA Modules:
  0.0 103.3 jit_solution(13080446717731867886)
XLA Ops:
  0.0 101.8 %shard_map.118 = bf16[8,5120]{1,0:T(8,128)(2,1)} custom-call(bf16[8,5120]{1,0:T(8,128)(2,1)} %hidden.1, bf16[2,8,5120]{2,1,0:T(8,128)(2,1)} %incoming.1, s32[1,16]{1,0:T(1,128)} %bitcast.15, bf16[3,96,5120]{2,1,0:T(8,128)(2,1)} %bitcast.12, bf16[320,5120]{1,0:T(8,128)(2,1)} %bitcast.8, bf16[320,5120]{1,0:T(8,128)(2,1)} %bitcast.9, ...), custom_call_target="tpu_custom_call" | custom-call | tf_op jit(solution)/shard_map/pallas_call | solution.py:695
  101.8 1.5 %copy.14 = bf16[8,5120]{1,0:T(8,128)(2,1)} copy(bf16[8,5120]{1,0:T(8,128)(2,1)} %shard_map.118) | data formatting | bytes 163840
